TPU v7x, 128 devices: a whole 4x4x4 slice. The times are simulated.
128 devices in a mesh: grp: 4 (over z), list: 32 (over y, x, core).
Axes of the slice: x: 4, y: 4, z: 4, core: 2. Of those that a mesh axis runs over, the one named last changes fastest.
Arguments:
- vectors: bfloat16 [3, 65536, 1024], P(None, ('grp', 'list')), may hold values from -6 to 6
- owner_route: int32 [3, 65536, 1], P(None, ('grp', 'list')), may hold values from 0 to 31; in each aligned block of 512 rows (0 to 511, 512 to 1023, ..., all dimensions but the last counted through in order) at most 32 rows name the same one
- list_slot: int32 [3, 65536], P(None, ('grp', 'list')), may hold values from 0 to 1023
- centroids: float32 [32768, 1024], P('list'), may hold values from -6 to 6
- counts: int32 [32768], P('list'), may hold values from 1 to 8
Outputs:
- residuals: bfloat16 [3, 65536, 1024], P(None, ('grp', 'list'))
- new_centroids: float32 [32768, 1024], P('list')
Inputs may be any that keep to these rules, and one draw needn't show every extreme that they name: `owner_route`: within the rows of one device for one step, at most 32 vectors name the same owner; some owner is named exactly 32 times.
All inputs are finite; a program needn't handle non-finite values.
Results may differ from a plain program's by a relative error of at most 0.0035.
Values may be sent and summed in bfloat16 or wider, within the bound.
No kernel may reach another device: no remote copies, remote signals or barrier semaphores. Data moves between devices by JAX's collectives and lax.ppermute only.
A program may use at most 128 MiB of HBM per device.

v0:
```python
import jax
import jax.numpy as jnp
from jax import lax
from jax.sharding import PartitionSpec as P

STEPS = 3


def list_sums(slots, rows, list_dev):
    one_hot = (jnp.arange(list_dev, dtype=jnp.int32)[:, None] == slots[None, :]).astype(
        jnp.bfloat16
    )
    sums = jnp.dot(one_hot, rows, preferred_element_type=jnp.float32)
    return (sums, jnp.sum(one_hot, axis=1, dtype=jnp.float32))


def local(vectors, owner_route, list_slot, centroids, counts):
    owner_count = lax.axis_size("list")
    row_count = vectors.shape[1]
    width = vectors.shape[2]
    capacity = 2 * row_count // owner_count
    list_dev = centroids.shape[0]
    current = centroids
    weights = counts.astype(jnp.float32)
    outputs = []
    for step_index in range(STEPS):
        owner_ids = owner_route[step_index, :, 0]
        slot_ids = list_slot[step_index]
        owner_hits = (
            owner_ids[:, None] == jnp.arange(owner_count, dtype=jnp.int32)[None, :]
        ).astype(jnp.int32)
        rank_rows = jnp.sum((jnp.cumsum(owner_hits, axis=0) - owner_hits) * owner_hits, axis=1)
        dest_rows = owner_ids * capacity + rank_rows
        send_rows = (
            jnp.zeros((owner_count * capacity, width), jnp.bfloat16)
            .at[dest_rows]
            .set(vectors[step_index])
        )
        send_rows = send_rows.reshape(owner_count, capacity, width)
        send_slots = jnp.full((owner_count * capacity,), -1, jnp.int32).at[dest_rows].set(slot_ids)
        send_slots = send_slots.reshape(owner_count, capacity)
        table = current

        def route_fn(pieces, table=table):
            vec_rows, list_ids = pieces
            chosen = table[jnp.clip(list_ids, 0, list_dev - 1)]
            residual_rows = (vec_rows.astype(jnp.float32) - chosen).astype(jnp.bfloat16)
            back_rows = lax.all_to_all(
                residual_rows, "list", split_axis=0, concat_axis=0, tiled=True
            )
            return (back_rows, vec_rows, list_ids)

        back_rows, recv_rows, recv_slots = route_fn(
            (
                lax.all_to_all(send_rows, "list", split_axis=0, concat_axis=0, tiled=True),
                lax.all_to_all(send_slots, "list", split_axis=0, concat_axis=0, tiled=True),
            )
        )
        outputs.append(back_rows.reshape(owner_count * capacity, width)[dest_rows])
        flat_rows = recv_rows.reshape(-1, width)
        flat_slots = recv_slots.reshape(-1)
        sums, batch_count = list_sums(flat_slots, flat_rows, list_dev)
        total_sums, total_count = (
            lax.psum(sums.astype(jnp.bfloat16), "grp").astype(jnp.float32),
            lax.psum(batch_count.astype(jnp.bfloat16), "grp").astype(jnp.float32),
        )
        current = (weights[:, None] * current + total_sums) / (weights + total_count)[:, None]
        weights = weights + total_count
    return (jnp.stack(outputs, axis=0), current)


def solution(mesh):
    in_specs = (
        P(None, ("grp", "list"), None),
        P(None, ("grp", "list"), None),
        P(None, ("grp", "list")),
        P("list", None),
        P("list"),
    )
    out_specs = (P(None, ("grp", "list"), None), P("list", None))
    return jax.shard_map(local, mesh=mesh, in_specs=in_specs, out_specs=out_specs, check_vma=False)
```

profile of v0, /device:TPU:0, one launch (start us, length us, event | category | flops | bytes accessed | tf_op | source)
XLA Modules:
  0.0 397.1 jit_solution(9526469417952136260)
XLA Ops:
  7.2 0.8 fusion.46
  8.0 0.7 fusion.47
  8.7 1.2 reduce-window.24
  10.2 1.2 reduce-window.20
  11.6 1.2 reduce-window.26
  13.4 0.7 compare_select_fusion.3
  14.1 2.4 scatter_custom_fusion.3
  17.2 7.4 %all-to-all-start.4 = ((s32[32,1,32]{2,1,0:T(1,128)}), s32[32,1,32]{2,1,0:T(1,128)S(1)}, u32[]{:S(2)}, u32[]{:S(2)}) async-start(s32[32,1,32]{2,1,0:T(1,128)} %all_to_all.41), calls=%async_computation.4 | async-start | bytes 32768 | tf_op jit(solution)/shard_map/all_to_all | solution.py:56
  24.6 2.4 scatter_custom_fusion.5
  27.8 4.1 %all-to-all-done.4 = s32[32,1,32]{2,1,0:T(1,128)S(1)} async-done(((s32[32,1,32]{2,1,0:T(1,128)}), s32[32,1,32]{2,1,0:T(1,128)S(1)}, u32[]{:S(2)}, u32[]{:S(2)}) %all-to-all-start.4) | async-done | bytes 4128 | tf_op jit(solution)/shard_map/all_to_all | solution.py:56
  31.9 3.9 all-to-all-start.7
  35.8 2.4 scatter_custom_fusion.1
  38.2 0.7 all_to_all.37
  38.9 4.2 %all-to-all-done.7 = s32[32,1,32]{2,1,0:T(1,128)S(1)} async-done(((s32[32,1,32]{2,1,0:T(1,128)}), s32[32,1,32]{2,1,0:T(1,128)S(1)}, u32[]{:S(2)}, u32[]{:S(2)}) %all-to-all-start.7) | async-done | bytes 4128 | tf_op jit(solution)/shard_map/all_to_all | solution.py:56
  43.1 3.8 all-to-all-start.1
  47.0 4.8 %scatter_custom_fusion.2 = bf16[1024,1024]{1,0:T(8,128)(2,1)} fusion(s32[512]{0:T(512)S(1)} %bitcast.152, bf16[3,512,1024]{2,1,0:T(8,128)(2,1)} %param.5, bf16[]{:T(256)} %constant.10.clone.1), kind=kCustom, calls=%fused_computation.39 | custom fusion | bytes 3146240 | tf_op jit(solution)/shard_map/scatter | solution.py:37
  51.8 2.5 all-to-all-done.1
  54.2 4.9 %all-to-all-start.3 = ((bf16[32,32,1024]{2,1,0:T(8,128)(2,1)}), bf16[32,32,1024]{2,1,0:T(8,128)(2,1)S(1)}, u32[]{:S(2)}, u32[]{:S(2)}) async-start(bf16[32,32,1024]{2,1,0:T(8,128)(2,1)} %bitcast.22), calls=%async_computation.3 | async-start | bytes 4194304 | tf_op jit(solution)/shard_map/all_to_all | solution.py:55
  59.2 4.8 %scatter_custom_fusion.4 = bf16[1024,1024]{1,0:T(8,128)(2,1)} fusion(s32[512]{0:T(512)S(1)} %bitcast.155, bf16[3,512,1024]{2,1,0:T(8,128)(2,1)} %param.5, bf16[]{:T(256)} %constant.10.clone.1), kind=kCustom, calls=%fused_computation.37 | custom fusion | bytes 3146240 | tf_op jit(solution)/shard_map/scatter | solution.py:37
  64.0 25.2 %all-to-all-done.3 = bf16[32,32,1024]{2,1,0:T(8,128)(2,1)S(1)} async-done(((bf16[32,32,1024]{2,1,0:T(8,128)(2,1)}), bf16[32,32,1024]{2,1,0:T(8,128)(2,1)S(1)}, u32[]{:S(2)}, u32[]{:S(2)}) %all-to-all-start.3) | async-done | bytes 2097184 | tf_op jit(solution)/shard_map/all_to_all | solution.py:55
  89.1 4.8 %all-to-all-start.6 = ((bf16[32,32,1024]{2,1,0:T(8,128)(2,1)}), bf16[32,32,1024]{2,1,0:T(8,128)(2,1)}, u32[]{:S(2)}, u32[]{:S(2)}) async-start(bf16[32,32,1024]{2,1,0:T(8,128)(2,1)} %bitcast.37), calls=%async_computation.6 | async-start | bytes 4194304 | tf_op jit(solution)/shard_map/all_to_all | solution.py:55
  93.9 4.8 %scatter_custom_fusion = bf16[1024,1024]{1,0:T(8,128)(2,1)} fusion(s32[512]{0:T(512)S(1)} %bitcast.158, bf16[3,512,1024]{2,1,0:T(8,128)(2,1)} %param.5, bf16[]{:T(256)} %constant.10.clone.1), kind=kCustom, calls=%fused_computation.41 | custom fusion | bytes 3146240 | tf_op jit(solution)/shard_map/scatter | solution.py:37
  98.7 25.2 %all-to-all-done.6 = bf16[32,32,1024]{2,1,0:T(8,128)(2,1)} async-done(((bf16[32,32,1024]{2,1,0:T(8,128)(2,1)}), bf16[32,32,1024]{2,1,0:T(8,128)(2,1)}, u32[]{:S(2)}, u32[]{:S(2)}) %all-to-all-start.6) | async-done | bytes 2097184 | tf_op jit(solution)/shard_map/all_to_all | solution.py:55
  123.9 4.8 %all-to-all-start = ((bf16[32,32,1024]{2,1,0:T(8,128)(2,1)}), bf16[32,32,1024]{2,1,0:T(8,128)(2,1)}, u32[]{:S(2)}, u32[]{:S(2)}) async-start(bf16[32,32,1024]{2,1,0:T(8,128)(2,1)} %bitcast.7), calls=%async_computation | async-start | bytes 4194304 | tf_op jit(solution)/shard_map/all_to_all | solution.py:55
  129.2 0.7 fusion.45
  131.6 3.7 fusion.13
  135.2 5.3 %fusion.14 = bf16[1024,1024]{1,0:T(8,128)(2,1)} fusion(bf16[1024,1024]{1,0:T(8,128)(2,1)} %bitcast.45, s32[1024]{0:T(1024)S(1)} %eq.153), kind=kOutput, calls=%fused_computation.36 | convolution fusion | flops 2149580800 | bytes 4198400 | tf_op jit(solution)/shard_map/dot_general | solution.py:13
  140.5 18.1 %all-to-all-done = bf16[32,32,1024]{2,1,0:T(8,128)(2,1)} async-done(((bf16[32,32,1024]{2,1,0:T(8,128)(2,1)}), bf16[32,32,1024]{2,1,0:T(8,128)(2,1)}, u32[]{:S(2)}, u32[]{:S(2)}) %all-to-all-start) | async-done | bytes 2097184 | tf_op jit(solution)/shard_map/all_to_all | solution.py:55
  158.6 5.2 %fusion.12 = bf16[1024,1024]{1,0:T(8,128)(2,1)} fusion(bf16[1024,1024]{1,0:T(8,128)(2,1)} %bitcast.23, s32[1024]{0:T(1024)S(1)} %eq.137), kind=kOutput, calls=%fused_computation.34 | convolution fusion | flops 2149580800 | bytes 4198400 | tf_op jit(solution)/shard_map/dot_general | solution.py:13
  164.7 8.5 %gather_fusion = f32[1024,1024]{1,0:T(8,128)} fusion(f32[1024,1024]{1,0:T(8,128)} %param.8, s32[1024]{0:T(1024)S(1)} %broadcast_clamp_fusion.2), kind=kCustom, calls=%fused_computation | custom fusion | bytes 8392704 | tf_op jit(solution)/shard_map/gather | solution.py:46
  173.7 1.0 fusion.6
  174.7 12.1 %all-reduce = (bf16[1024]{0:T(1024)(128)(2,1)S(1)}, bf16[1024]{0:T(1024)(128)(2,1)S(1)}, bf16[1024]{0:T(1024)(128)(2,1)S(1)}) all-reduce(bf16[1024]{0:T(1024)(128)(2,1)S(1)} %get-tuple-element.25, bf16[1024]{0:T(1024)(128)(2,1)S(1)} %get-tuple-element.26, bf16[1024]{0:T(1024)(128)(2,1)S(1)} %fusion.8), channel_id=1, replica_groups=mesh['grp'=4,'list'=32] {'grp'}, use_global_device_ids=true, to_apply=%region_11.12 | all-reduce | flops 3072 | bytes 12288 | tf_op jit(solution)/shard_map/psum | solution.py:65
  186.9 5.1 %subtract_convert_fusion.2 = bf16[32,32,1024]{2,1,0:T(8,128)(2,1)} fusion(f32[32,32,1024]{2,1,0:T(8,128)} %bitcast.133, bf16[32,32,1024]{2,1,0:T(8,128)(2,1)} %all-to-all-done), kind=kLoop, calls=%fused_computation.26 | loop fusion | flops 3145728 | bytes 8388608 | tf_op jit(solution)/shard_map/convert_element_type | solution.py:47
  192.0 4.2 %all-to-all-start.2 = ((bf16[32,32,1024]{2,1,0:T(8,128)(2,1)}), bf16[32,32,1024]{2,1,0:T(8,128)(2,1)S(1)}, u32[]{:S(2)}, u32[]{:S(2)}) async-start(bf16[32,32,1024]{2,1,0:T(8,128)(2,1)} %subtract_convert_fusion.2), calls=%async_computation.2 | async-start | bytes 4194304 | tf_op jit(solution)/shard_map/all_to_all | solution.py:48
  196.3 93.5 %all-reduce.4.cloned.1.call-done = (bf16[1024,1024]{1,0:T(8,128)(2,1)}, bf16[1024,1024]{1,0:T(8,128)(2,1)}, bf16[1024,1024]{1,0:T(8,128)(2,1)}) async-done(((bf16[1024,1024]{1,0:T(8,128)(2,1)}, bf16[1024,1024]{1,0:T(8,128)(2,1)}, bf16[1024,1024]{1,0:T(8,128)(2,1)}), (bf16[1024,1024]{1,0:T(8,128)(2,1)}, bf16[1024,1024]{1,0:T(8,128)(2,1)}, bf16[1024,1024]{1,0:T(8,128)(2,1)})) %all-reduce.4.cloned.1.call-update) | async-done | bytes 6291472 | tf_op jit(solution)/shard_map/psum | solution.py:64
  289.7 8.4 %add_divide_fusion = (f32[1024,1024]{1,0:T(8,128)}, f32[1024,1024]{1,0:T(8,128)}, f32[1024,1024]{1,0:T(8,128)}) fusion(bf16[1024,1024]{1,0:T(8,128)(2,1)} %get-tuple-element.7, f32[1024]{0:T(1024)S(1)} %get-tuple-element.11, f32[1024]{0:T(1024)S(1)} %get-tuple-element.12, bf16[1024,1024]{1,0:T(8,128)(2,1)} %get-tuple-element.5, ...), kind=kLoop, calls=%fused_computation.12 | loop fusion | flops 12582912 | bytes 23085056 | tf_op jit(solution)/shard_map/div | solution.py:67
  298.1 8.6 %gather_fusion.4 = f32[1024,1024]{1,0:T(8,128)} fusion(f32[1024,1024]{1,0:T(8,128)} %get-tuple-element.9, s32[1024]{0:T(1024)S(1)} %broadcast_clamp_fusion), kind=kCustom, calls=%fused_computation.4 | custom fusion | bytes 8392704 | tf_op jit(solution)/shard_map/gather | solution.py:46
  306.7 5.0 %subtract_convert_fusion = bf16[32,32,1024]{2,1,0:T(8,128)(2,1)} fusion(f32[32,32,1024]{2,1,0:T(8,128)} %bitcast.134, bf16[32,32,1024]{2,1,0:T(8,128)(2,1)} %all-to-all-done.6), kind=kLoop, calls=%fused_computation.16 | loop fusion | flops 3145728 | bytes 8388608 | tf_op jit(solution)/shard_map/convert_element_type | solution.py:47
  311.7 7.2 %all-to-all-start.8 = ((bf16[32,32,1024]{2,1,0:T(8,128)(2,1)}), bf16[32,32,1024]{2,1,0:T(8,128)(2,1)}, u32[]{:S(2)}, u32[]{:S(2)}) async-start(bf16[32,32,1024]{2,1,0:T(8,128)(2,1)} %subtract_convert_fusion), calls=%async_computation.8 | async-start | bytes 4194304 | tf_op jit(solution)/shard_map/all_to_all | solution.py:48
  319.0 8.6 %gather_fusion.2 = f32[1024,1024]{1,0:T(8,128)} fusion(f32[1024,1024]{1,0:T(8,128)} %get-tuple-element.10, s32[1024]{0:T(1024)S(1)} %broadcast_clamp_fusion.1), kind=kCustom, calls=%fused_computation.2 | custom fusion | bytes 8392704 | tf_op jit(solution)/shard_map/gather | solution.py:46
  327.6 5.0 %subtract_convert_fusion.1 = bf16[32,32,1024]{2,1,0:T(8,128)(2,1)} fusion(f32[32,32,1024]{2,1,0:T(8,128)} %bitcast.135, bf16[32,32,1024]{2,1,0:T(8,128)(2,1)} %copy-done), kind=kLoop, calls=%fused_computation.21 | loop fusion | flops 3145728 | bytes 8388608 | tf_op jit(solution)/shard_map/convert_element_type | solution.py:47
  332.6 16.3 %all-to-all-done.8 = bf16[32,32,1024]{2,1,0:T(8,128)(2,1)} async-done(((bf16[32,32,1024]{2,1,0:T(8,128)(2,1)}), bf16[32,32,1024]{2,1,0:T(8,128)(2,1)}, u32[]{:S(2)}, u32[]{:S(2)}) %all-to-all-start.8) | async-done | bytes 2097184 | tf_op jit(solution)/shard_map/all_to_all | solution.py:48
  348.9 4.8 %all-to-all-start.5 = ((bf16[32,32,1024]{2,1,0:T(8,128)(2,1)}), bf16[32,32,1024]{2,1,0:T(8,128)(2,1)}, u32[]{:S(2)}, u32[]{:S(2)}) async-start(bf16[32,32,1024]{2,1,0:T(8,128)(2,1)} %subtract_convert_fusion.1), calls=%async_computation.5 | async-start | bytes 4194304 | tf_op jit(solution)/shard_map/all_to_all | solution.py:48
  353.7 2.1 gather_fusion.1
  355.8 4.6 %gather_fusion.5 = bf16[512,1024]{1,0:T(8,128)(2,1)S(1)} fusion(bf16[1024,1024]{1,0:T(8,128)(2,1)} %bitcast.43, s32[1024]{0:T(1024)S(1)} %pad_clamp_fusion), kind=kCustom, calls=%fused_computation.5 | custom fusion | bytes 2099200 | tf_op jit(solution)/shard_map/gather | solution.py:59
  360.4 23.3 %all-to-all-done.5 = bf16[32,32,1024]{2,1,0:T(8,128)(2,1)} async-done(((bf16[32,32,1024]{2,1,0:T(8,128)(2,1)}), bf16[32,32,1024]{2,1,0:T(8,128)(2,1)}, u32[]{:S(2)}, u32[]{:S(2)}) %all-to-all-start.5) | async-done | bytes 2097184 | tf_op jit(solution)/shard_map/all_to_all | solution.py:48
  383.6 4.6 %gather_fusion.3 = bf16[512,1024]{1,0:T(8,128)(2,1)S(1)} fusion(bf16[1024,1024]{1,0:T(8,128)(2,1)} %bitcast.28, s32[1024]{0:T(1024)S(1)} %pad_clamp_fusion.1), kind=kCustom, calls=%fused_computation.3 | custom fusion | bytes 2099200 | tf_op jit(solution)/shard_map/gather | solution.py:59
  388.2 2.0 pad_maximum_fusion
  (47 shorter events, 6.1 us)
Async XLA Ops:
  17.2 14.7 %all-to-all-start.4 = ((s32[32,1,32]{2,1,0:T(1,128)}), s32[32,1,32]{2,1,0:T(1,128)S(1)}, u32[]{:S(2)}, u32[]{:S(2)}) async-start(s32[32,1,32]{2,1,0:T(1,128)} %all_to_all.41), calls=%async_computation.4 | async-start | bytes 32768 | tf_op jit(solution)/shard_map/all_to_all | solution.py:56
  31.9 11.2 %all-to-all-start.7 = ((s32[32,1,32]{2,1,0:T(1,128)}), s32[32,1,32]{2,1,0:T(1,128)S(1)}, u32[]{:S(2)}, u32[]{:S(2)}) async-start(s32[32,1,32]{2,1,0:T(1,128)} %all_to_all.45), calls=%async_computation.7 | async-start | bytes 32768 | tf_op jit(solution)/shard_map/all_to_all | solution.py:56
  43.1 11.1 %all-to-all-start.1 = ((s32[32,1,32]{2,1,0:T(1,128)}), s32[32,1,32]{2,1,0:T(1,128)S(1)}, u32[]{:S(2)}, u32[]{:S(2)}) async-start(s32[32,1,32]{2,1,0:T(1,128)} %all_to_all.37), calls=%async_computation.1 | async-start | bytes 32768 | tf_op jit(solution)/shard_map/all_to_all | solution.py:56
  54.2 34.9 %all-to-all-start.3 = ((bf16[32,32,1024]{2,1,0:T(8,128)(2,1)}), bf16[32,32,1024]{2,1,0:T(8,128)(2,1)S(1)}, u32[]{:S(2)}, u32[]{:S(2)}) async-start(bf16[32,32,1024]{2,1,0:T(8,128)(2,1)} %bitcast.22), calls=%async_computation.3 | async-start | bytes 4194304 | tf_op jit(solution)/shard_map/all_to_all | solution.py:55
  89.1 42.4 %copy-start = (bf16[32,32,1024]{2,1,0:T(8,128)(2,1)}, bf16[32,32,1024]{2,1,0:T(8,128)(2,1)S(1)}, u32[]{:S(2)}) copy-start(bf16[32,32,1024]{2,1,0:T(8,128)(2,1)S(1)} %all-to-all-done.3) | copy-start | bytes 6291460
  89.1 34.7 %all-to-all-start.6 = ((bf16[32,32,1024]{2,1,0:T(8,128)(2,1)}), bf16[32,32,1024]{2,1,0:T(8,128)(2,1)}, u32[]{:S(2)}, u32[]{:S(2)}) async-start(bf16[32,32,1024]{2,1,0:T(8,128)(2,1)} %bitcast.37), calls=%async_computation.6 | async-start | bytes 4194304 | tf_op jit(solution)/shard_map/all_to_all | solution.py:55
  123.9 34.7 %all-to-all-start = ((bf16[32,32,1024]{2,1,0:T(8,128)(2,1)}), bf16[32,32,1024]{2,1,0:T(8,128)(2,1)}, u32[]{:S(2)}, u32[]{:S(2)}) async-start(bf16[32,32,1024]{2,1,0:T(8,128)(2,1)} %bitcast.7), calls=%async_computation | async-start | bytes 4194304 | tf_op jit(solution)/shard_map/all_to_all | solution.py:55
  128.6 161.1 %all-reduce.4.cloned.1.call-start = ((), (), s32[]{:S(2)}) async-start(), calls=%async_computation.9 | async-start | bytes 12582912 | tf_op jit(solution)/shard_map/psum | solution.py:64
  163.8 0.7 copy-start.1
  192.0 119.7 %all-to-all-start.2 = ((bf16[32,32,1024]{2,1,0:T(8,128)(2,1)}), bf16[32,32,1024]{2,1,0:T(8,128)(2,1)S(1)}, u32[]{:S(2)}, u32[]{:S(2)}) async-start(bf16[32,32,1024]{2,1,0:T(8,128)(2,1)} %subtract_convert_fusion.2), calls=%async_computation.2 | async-start | bytes 4194304 | tf_op jit(solution)/shard_map/all_to_all | solution.py:48
  311.7 37.2 %all-to-all-start.8 = ((bf16[32,32,1024]{2,1,0:T(8,128)(2,1)}), bf16[32,32,1024]{2,1,0:T(8,128)(2,1)}, u32[]{:S(2)}, u32[]{:S(2)}) async-start(bf16[32,32,1024]{2,1,0:T(8,128)(2,1)} %subtract_convert_fusion), calls=%async_computation.8 | async-start | bytes 4194304 | tf_op jit(solution)/shard_map/all_to_all | solution.py:48
  348.9 34.7 %all-to-all-start.5 = ((bf16[32,32,1024]{2,1,0:T(8,128)(2,1)}), bf16[32,32,1024]{2,1,0:T(8,128)(2,1)}, u32[]{:S(2)}, u32[]{:S(2)}) async-start(bf16[32,32,1024]{2,1,0:T(8,128)(2,1)} %subtract_convert_fusion.1), calls=%async_computation.5 | async-start | bytes 4194304 | tf_op jit(solution)/shard_map/all_to_all | solution.py:48
Sparse Core Ops, SparseCore 0:
  164.0 125.7 all-reduce.3
where the time goes:
time: 398 us; the launch traced here: 397 us
  waiting for transfers between devices  212 us (53%)
  local copies, waits for them, and re-layouts  64.6 us (16%)
  starting transfers between devices  45.8 us (12%)
  other arithmetic  33.8 us (8%)
  between operations  14.3 us (4%)
  matrix products  14.1 us (4%)
  blocking collectives  12.1 us (3%)
    psum x1, waiting for transfers between devices, local(): lax.psum(sums.astype(jnp.bfloat16), 'grp').astype(jnp.float32)  93.5 us
    all_to_all x3, waiting for transfers between devices, local(): lax.all_to_all(send_rows, 'list', split_axis=0, concat_axis=0, tiled=True)  68.5 us
    all_to_all x3, waiting for transfers between devices, route_fn(): lax.all_to_all(residual_rows, 'list', split_axis=0, concat_axis=0, tiled=...  39.6 us
    gather x3, local copies, waits for them, and re-layouts, route_fn(): chosen = table[jnp.clip(list_ids, 0, list_dev - 1)]  25.8 us
    all_to_all x3, starting transfers between devices, route_fn(): lax.all_to_all(residual_rows, 'list', split_axis=0, concat_axis=0, tiled=...  16.2 us
    all_to_all x3, starting transfers between devices, local(): lax.all_to_all(send_slots, 'list', split_axis=0, concat_axis=0, tiled=True)  15.1 us
    convert_element_type x3, other arithmetic, route_fn(): residual_rows = (vec_rows.astype(jnp.float32) - chosen).astype(jnp.bfloat16)  15.1 us
    all_to_all x3, starting transfers between devices, local(): lax.all_to_all(send_rows, 'list', split_axis=0, concat_axis=0, tiled=True)  14.4 us
  transfers between devices with their start and end apart: 10, of which 9 were waited for; matrix products, arithmetic and copies ran while one was open for 22% of the time, Pallas kernels for 0%

commit v1 on v0

--- a/solution.py
+++ b/solution.py
@@ -61,7 +61,7 @@
         flat_slots = recv_slots.reshape(-1)
         sums, batch_count = list_sums(flat_slots, flat_rows, list_dev)
         total_sums, total_count = (
-            lax.psum(sums.astype(jnp.bfloat16), "grp").astype(jnp.float32),
+            jnp.sum(lax.all_gather(sums.astype(jnp.bfloat16), "grp"), axis=0).astype(jnp.float32),
             lax.psum(batch_count.astype(jnp.bfloat16), "grp").astype(jnp.float32),
         )
         current = (weights[:, None] * current + total_sums) / (weights + total_count)[:, None]

time: 398 us -> 448 us (1.13); the launches traced: 397 us -> 439 us
  waiting for transfers between devices: 212 us -> 236 us
  other arithmetic: 33.8 us -> 55.4 us
    all_gather x0 -> x3, waiting for transfers between devices: none -> 102 us  [local(): lax.all_gather(sums.astype(jnp.bfloat16), 'grp')]
    psum x1 -> x0, waiting for transfers between devices: 93.5 us -> none  [local(): lax.psum(sums.astype(jnp.bfloat16), 'grp').astype(jnp.float32)]
    reduce_sum x0 -> x3, other arithmetic: none -> 22.4 us  [local(): jnp.sum(lax.all_gather(sums.astype(jnp.bfloat16), 'grp'), axis=0)]
    all_to_all x3, waiting for transfers between devices: 68.5 us -> 87 us  [local(): lax.all_to_all(send_rows, 'list', split_axis=0, concat_axis=0, tiled=True)]
  transfers between devices with their start and end apart: 10 -> 12, of which waited for: 9 -> 10; matrix products, arithmetic and copies ran while one was open for 22% -> 25% of each run, Pallas kernels for 0% -> 0%
where the time goes in v1:
time: 448 us; the launch traced here: 439 us
  waiting for transfers between devices  236 us (53%)
  local copies, waits for them, and re-layouts  64.2 us (14%)
  other arithmetic  55.4 us (12%)
  starting transfers between devices  46.5 us (10%)
  between operations  14.5 us (3%)
  blocking collectives  12.1 us (3%)
  matrix products  10.9 us (2%)
    all_gather x3, waiting for transfers between devices, local(): lax.all_gather(sums.astype(jnp.bfloat16), 'grp')  102 us
    all_to_all x3, waiting for transfers between devices, local(): lax.all_to_all(send_rows, 'list', split_axis=0, concat_axis=0, tiled=True)  87 us
    all_to_all x3, waiting for transfers between devices, route_fn(): lax.all_to_all(residual_rows, 'list', split_axis=0, concat_axis=0, tiled=...  39.5 us
    gather x3, local copies, waits for them, and re-layouts, route_fn(): chosen = table[jnp.clip(list_ids, 0, list_dev - 1)]  25.8 us
    reduce_sum x3, other arithmetic, local(): jnp.sum(lax.all_gather(sums.astype(jnp.bfloat16), 'grp'), axis=0)  22.4 us
    all_to_all x3, starting transfers between devices, route_fn(): lax.all_to_all(residual_rows, 'list', split_axis=0, concat_axis=0, tiled=...  16.5 us
    all_to_all x3, starting transfers between devices, local(): lax.all_to_all(send_slots, 'list', split_axis=0, concat_axis=0, tiled=True)  15.2 us
    all_to_all x3, starting transfers between devices, local(): lax.all_to_all(send_rows, 'list', split_axis=0, concat_axis=0, tiled=True)  14.8 us
  transfers between devices with their start and end apart: 12, of which 10 were waited for; matrix products, arithmetic and copies ran while one was open for 25% of the time, Pallas kernels for 0%

profile of v1, /device:TPU:0, one launch (start us, length us, event | category | flops | bytes accessed | tf_op | source)
XLA Modules:
  0.0 439.3 jit_solution(10190316532154573034)
XLA Ops:
  7.2 0.8 fusion.46
  8.7 1.2 reduce-window.26
  10.2 1.2 reduce-window.20
  11.6 1.2 reduce-window.24
  13.4 0.7 compare_select_fusion.4
  14.1 2.4 scatter_custom_fusion.5
  17.2 7.4 %all-to-all-start.7 = ((s32[32,1,32]{2,1,0:T(1,128)}), s32[32,1,32]{2,1,0:T(1,128)S(1)}, u32[]{:S(2)}, u32[]{:S(2)}) async-start(s32[32,1,32]{2,1,0:T(1,128)} %all_to_all.45), calls=%async_computation.7 | async-start | bytes 32768 | tf_op jit(solution)/shard_map/all_to_all | solution.py:56
  24.6 4.8 %scatter_custom_fusion.4 = bf16[1024,1024]{1,0:T(8,128)(2,1)} fusion(s32[512]{0:T(512)S(1)} %bitcast.160, bf16[3,512,1024]{2,1,0:T(8,128)(2,1)} %param.5, bf16[]{:T(256)} %constant.24.clone.1), kind=kCustom, calls=%fused_computation.37 | custom fusion | bytes 3146240 | tf_op jit(solution)/shard_map/scatter | solution.py:37
  29.4 2.5 all-to-all-done.7
  31.9 4.9 %all-to-all-start.6 = ((bf16[32,32,1024]{2,1,0:T(8,128)(2,1)}), bf16[32,32,1024]{2,1,0:T(8,128)(2,1)S(1)}, u32[]{:S(2)}, u32[]{:S(2)}) async-start(bf16[32,32,1024]{2,1,0:T(8,128)(2,1)} %bitcast.38), calls=%async_computation.6 | async-start | bytes 4194304 | tf_op jit(solution)/shard_map/all_to_all | solution.py:55
  38.1 28.7 %all-to-all-done.6 = bf16[32,32,1024]{2,1,0:T(8,128)(2,1)S(1)} async-done(((bf16[32,32,1024]{2,1,0:T(8,128)(2,1)}), bf16[32,32,1024]{2,1,0:T(8,128)(2,1)S(1)}, u32[]{:S(2)}, u32[]{:S(2)}) %all-to-all-start.6) | async-done | bytes 2097184 | tf_op jit(solution)/shard_map/all_to_all | solution.py:55
  66.8 3.7 fusion.14
  70.5 2.4 scatter_custom_fusion.3
  73.6 3.9 all-to-all-start.4
  77.6 4.9 %scatter_custom_fusion.2 = bf16[1024,1024]{1,0:T(8,128)(2,1)} fusion(s32[512]{0:T(512)S(1)} %bitcast.163, bf16[3,512,1024]{2,1,0:T(8,128)(2,1)} %param.5, bf16[]{:T(256)} %constant.24.clone.1), kind=kCustom, calls=%fused_computation.39 | custom fusion | bytes 3146240 | tf_op jit(solution)/shard_map/scatter | solution.py:37
  82.5 2.5 all-to-all-done.4
  85.0 5.0 %all-to-all-start.3 = ((bf16[32,32,1024]{2,1,0:T(8,128)(2,1)}), bf16[32,32,1024]{2,1,0:T(8,128)(2,1)S(1)}, u32[]{:S(2)}, u32[]{:S(2)}) async-start(bf16[32,32,1024]{2,1,0:T(8,128)(2,1)} %bitcast.22), calls=%async_computation.3 | async-start | bytes 4194304 | tf_op jit(solution)/shard_map/all_to_all | solution.py:55
  90.8 29.2 %all-to-all-done.3 = bf16[32,32,1024]{2,1,0:T(8,128)(2,1)S(1)} async-done(((bf16[32,32,1024]{2,1,0:T(8,128)(2,1)}), bf16[32,32,1024]{2,1,0:T(8,128)(2,1)S(1)}, u32[]{:S(2)}, u32[]{:S(2)}) %all-to-all-start.3) | async-done | bytes 2097184 | tf_op jit(solution)/shard_map/all_to_all | solution.py:55
  120.0 3.7 fusion.13
  123.7 2.4 scatter_custom_fusion.1
  126.8 3.8 all-to-all-start.1
  130.6 4.8 %scatter_custom_fusion = bf16[1024,1024]{1,0:T(8,128)(2,1)} fusion(s32[512]{0:T(512)S(1)} %bitcast.166, bf16[3,512,1024]{2,1,0:T(8,128)(2,1)} %param.5, bf16[]{:T(256)} %constant.24.clone.1), kind=kCustom, calls=%fused_computation.41 | custom fusion | bytes 3146240 | tf_op jit(solution)/shard_map/scatter | solution.py:37
  135.5 2.5 all-to-all-done.1
  138.0 4.8 %all-to-all-start = ((bf16[32,32,1024]{2,1,0:T(8,128)(2,1)}), bf16[32,32,1024]{2,1,0:T(8,128)(2,1)S(1)}, u32[]{:S(2)}, u32[]{:S(2)}) async-start(bf16[32,32,1024]{2,1,0:T(8,128)(2,1)} %bitcast.7), calls=%async_computation | async-start | bytes 4194304 | tf_op jit(solution)/shard_map/all_to_all | solution.py:55
  143.7 29.2 %all-to-all-done = bf16[32,32,1024]{2,1,0:T(8,128)(2,1)S(1)} async-done(((bf16[32,32,1024]{2,1,0:T(8,128)(2,1)}), bf16[32,32,1024]{2,1,0:T(8,128)(2,1)S(1)}, u32[]{:S(2)}, u32[]{:S(2)}) %all-to-all-start) | async-done | bytes 2097184 | tf_op jit(solution)/shard_map/all_to_all | solution.py:55
  172.8 3.6 fusion.12
  176.7 8.6 %gather_fusion = f32[1024,1024]{1,0:T(8,128)} fusion(f32[1024,1024]{1,0:T(8,128)} %param.8, s32[1024]{0:T(1024)S(1)} %broadcast_clamp_fusion.2), kind=kCustom, calls=%fused_computation | custom fusion | bytes 8392704 | tf_op jit(solution)/shard_map/gather | solution.py:46
  186.8 12.1 %all-reduce = (bf16[1024]{0:T(1024)(128)(2,1)S(1)}, bf16[1024]{0:T(1024)(128)(2,1)S(1)}, bf16[1024]{0:T(1024)(128)(2,1)S(1)}) all-reduce(bf16[1024]{0:T(1024)(128)(2,1)S(1)} %fusion.6, bf16[1024]{0:T(1024)(128)(2,1)S(1)} %fusion.7, bf16[1024]{0:T(1024)(128)(2,1)S(1)} %fusion.8), channel_id=1, replica_groups=mesh['grp'=4,'list'=32] {'grp'}, use_global_device_ids=true, to_apply=%region_11.12 | all-reduce | flops 3072 | bytes 12288 | tf_op jit(solution)/shard_map/psum | solution.py:65
  198.9 4.4 %subtract_convert_fusion.2 = bf16[32,32,1024]{2,1,0:T(8,128)(2,1)} fusion(f32[32,32,1024]{2,1,0:T(8,128)} %bitcast.136, bf16[32,32,1024]{2,1,0:T(8,128)(2,1)S(1)} %all-to-all-done), kind=kLoop, calls=%fused_computation.26 | loop fusion | flops 3145728 | bytes 8388608 | tf_op jit(solution)/shard_map/convert_element_type | solution.py:47
  203.4 4.2 all-to-all-start.2
  207.6 7.4 %reduce_sum.115 = bf16[1024,1024]{1,0:T(8,128)(2,1)} reduce(bf16[4,1024,1024]{2,1,0:T(8,128)(2,1)} %bitcast.139, bf16[]{:T(256)} %constant.24.clone.1), dimensions={0}, to_apply=%region_21.22 | reduce | flops 3145728 | bytes 10485762 | tf_op jit(solution)/shard_map/reduce_sum | solution.py:64
  215.1 23.3 %all-gather.9.cloned.1.call-done = bf16[4096,1024]{1,0:T(8,128)(2,1)} async-done(((bf16[1024,1024]{1,0:T(8,128)(2,1)}), bf16[4096,1024]{1,0:T(8,128)(2,1)}) %all-gather.9.cloned.1.call-update) | async-done | bytes 8388624 | tf_op jit(solution)/shard_map/all_gather | solution.py:64
  238.4 7.4 %reduce_sum.113 = bf16[1024,1024]{1,0:T(8,128)(2,1)} reduce(bf16[4,1024,1024]{2,1,0:T(8,128)(2,1)} %bitcast.140, bf16[]{:T(256)} %constant.24.clone.1), dimensions={0}, to_apply=%region_17.18 | reduce | flops 3145728 | bytes 10485762 | tf_op jit(solution)/shard_map/reduce_sum | solution.py:64
  245.8 78.2 %all-gather.7.cloned.1.call-done = bf16[4096,1024]{1,0:T(8,128)(2,1)} async-done(((bf16[1024,1024]{1,0:T(8,128)(2,1)}), bf16[4096,1024]{1,0:T(8,128)(2,1)}) %all-gather.7.cloned.1.call-update) | async-done | bytes 8388624 | tf_op jit(solution)/shard_map/all_gather | solution.py:64
  324.0 7.5 %reduce_sum.109 = bf16[1024,1024]{1,0:T(8,128)(2,1)} reduce(bf16[4,1024,1024]{2,1,0:T(8,128)(2,1)} %bitcast.141, bf16[]{:T(256)} %constant.24.clone.1), dimensions={0}, to_apply=%region_9.10 | reduce | flops 3145728 | bytes 10485762 | tf_op jit(solution)/shard_map/reduce_sum | solution.py:64
  331.6 8.4 %add_divide_fusion = (f32[1024,1024]{1,0:T(8,128)}, f32[1024,1024]{1,0:T(8,128)}, f32[1024,1024]{1,0:T(8,128)}) fusion(bf16[1024,1024]{1,0:T(8,128)(2,1)} %reduce_sum.115, f32[1024]{0:T(1024)S(1)} %get-tuple-element.8, f32[1024]{0:T(1024)S(1)} %get-tuple-element.9, bf16[1024,1024]{1,0:T(8,128)(2,1)} %reduce_sum.113, f32[1024]{0:T(1024)S(1)} %get-tuple-element.10, ...), kind=kLoop, calls=%fused_computation.12 | loop fusion | flops 12582912 | bytes 23085056 | tf_op jit(solution)/shard_map/div | solution.py:67
  339.9 8.6 %gather_fusion.4 = f32[1024,1024]{1,0:T(8,128)} fusion(f32[1024,1024]{1,0:T(8,128)} %get-tuple-element.6, s32[1024]{0:T(1024)S(1)} %broadcast_clamp_fusion), kind=kCustom, calls=%fused_computation.4 | custom fusion | bytes 8392704 | tf_op jit(solution)/shard_map/gather | solution.py:46
  348.5 5.0 %subtract_convert_fusion = bf16[32,32,1024]{2,1,0:T(8,128)(2,1)} fusion(f32[32,32,1024]{2,1,0:T(8,128)} %bitcast.137, bf16[32,32,1024]{2,1,0:T(8,128)(2,1)} %copy-done), kind=kLoop, calls=%fused_computation.16 | loop fusion | flops 3145728 | bytes 8388608 | tf_op jit(solution)/shard_map/convert_element_type | solution.py:47
  353.5 7.5 %all-to-all-start.8 = ((bf16[32,32,1024]{2,1,0:T(8,128)(2,1)}), bf16[32,32,1024]{2,1,0:T(8,128)(2,1)}, u32[]{:S(2)}, u32[]{:S(2)}) async-start(bf16[32,32,1024]{2,1,0:T(8,128)(2,1)} %subtract_convert_fusion), calls=%async_computation.8 | async-start | bytes 4194304 | tf_op jit(solution)/shard_map/all_to_all | solution.py:48
  361.1 8.6 %gather_fusion.2 = f32[1024,1024]{1,0:T(8,128)} fusion(f32[1024,1024]{1,0:T(8,128)} %get-tuple-element.7, s32[1024]{0:T(1024)S(1)} %broadcast_clamp_fusion.1), kind=kCustom, calls=%fused_computation.2 | custom fusion | bytes 8392704 | tf_op jit(solution)/shard_map/gather | solution.py:46
  369.7 5.0 %subtract_convert_fusion.1 = bf16[32,32,1024]{2,1,0:T(8,128)(2,1)} fusion(f32[32,32,1024]{2,1,0:T(8,128)} %bitcast.138, bf16[32,32,1024]{2,1,0:T(8,128)(2,1)} %copy-done.1), kind=kLoop, calls=%fused_computation.21 | loop fusion | flops 3145728 | bytes 8388608 | tf_op jit(solution)/shard_map/convert_element_type | solution.py:47
  374.7 16.2 %all-to-all-done.8 = bf16[32,32,1024]{2,1,0:T(8,128)(2,1)} async-done(((bf16[32,32,1024]{2,1,0:T(8,128)(2,1)}), bf16[32,32,1024]{2,1,0:T(8,128)(2,1)}, u32[]{:S(2)}, u32[]{:S(2)}) %all-to-all-start.8) | async-done | bytes 2097184 | tf_op jit(solution)/shard_map/all_to_all | solution.py:48
  391.0 4.8 %all-to-all-start.5 = ((bf16[32,32,1024]{2,1,0:T(8,128)(2,1)}), bf16[32,32,1024]{2,1,0:T(8,128)(2,1)}, u32[]{:S(2)}, u32[]{:S(2)}) async-start(bf16[32,32,1024]{2,1,0:T(8,128)(2,1)} %subtract_convert_fusion.1), calls=%async_computation.5 | async-start | bytes 4194304 | tf_op jit(solution)/shard_map/all_to_all | solution.py:48
  395.8 2.1 gather_fusion.1
  397.8 4.6 %gather_fusion.5 = bf16[512,1024]{1,0:T(8,128)(2,1)S(1)} fusion(bf16[1024,1024]{1,0:T(8,128)(2,1)} %bitcast.45, s32[1024]{0:T(1024)S(1)} %pad_clamp_fusion), kind=kCustom, calls=%fused_computation.5 | custom fusion | bytes 2099200 | tf_op jit(solution)/shard_map/gather | solution.py:59
  402.4 23.3 %all-to-all-done.5 = bf16[32,32,1024]{2,1,0:T(8,128)(2,1)} async-done(((bf16[32,32,1024]{2,1,0:T(8,128)(2,1)}), bf16[32,32,1024]{2,1,0:T(8,128)(2,1)}, u32[]{:S(2)}, u32[]{:S(2)}) %all-to-all-start.5) | async-done | bytes 2097184 | tf_op jit(solution)/shard_map/all_to_all | solution.py:48
  425.7 4.6 %gather_fusion.3 = bf16[512,1024]{1,0:T(8,128)(2,1)S(1)} fusion(bf16[1024,1024]{1,0:T(8,128)(2,1)} %bitcast.29, s32[1024]{0:T(1024)S(1)} %pad_clamp_fusion.1), kind=kCustom, calls=%fused_computation.3 | custom fusion | bytes 2099200 | tf_op jit(solution)/shard_map/gather | solution.py:59
  430.3 2.0 pad_maximum_fusion
  (59 shorter events, 8.6 us)
Async XLA Ops:
  17.2 14.7 %all-to-all-start.7 = ((s32[32,1,32]{2,1,0:T(1,128)}), s32[32,1,32]{2,1,0:T(1,128)S(1)}, u32[]{:S(2)}, u32[]{:S(2)}) async-start(s32[32,1,32]{2,1,0:T(1,128)} %all_to_all.45), calls=%async_computation.7 | async-start | bytes 32768 | tf_op jit(solution)/shard_map/all_to_all | solution.py:56
  31.9 34.9 %all-to-all-start.6 = ((bf16[32,32,1024]{2,1,0:T(8,128)(2,1)}), bf16[32,32,1024]{2,1,0:T(8,128)(2,1)S(1)}, u32[]{:S(2)}, u32[]{:S(2)}) async-start(bf16[32,32,1024]{2,1,0:T(8,128)(2,1)} %bitcast.38), calls=%async_computation.6 | async-start | bytes 4194304 | tf_op jit(solution)/shard_map/all_to_all | solution.py:55
  36.8 170.8 %all-gather.11.cloned.1.call-start = ((), (), s32[]{:S(2)}) async-start(), calls=%async_computation.11 | async-start | bytes 10485760 | tf_op jit(solution)/shard_map/all_gather | solution.py:64
  66.8 3.7 copy-start
  73.6 11.3 %all-to-all-start.4 = ((s32[32,1,32]{2,1,0:T(1,128)}), s32[32,1,32]{2,1,0:T(1,128)S(1)}, u32[]{:S(2)}, u32[]{:S(2)}) async-start(s32[32,1,32]{2,1,0:T(1,128)} %all_to_all.41), calls=%async_computation.4 | async-start | bytes 32768 | tf_op jit(solution)/shard_map/all_to_all | solution.py:56
  85.0 35.0 %all-to-all-start.3 = ((bf16[32,32,1024]{2,1,0:T(8,128)(2,1)}), bf16[32,32,1024]{2,1,0:T(8,128)(2,1)S(1)}, u32[]{:S(2)}, u32[]{:S(2)}) async-start(bf16[32,32,1024]{2,1,0:T(8,128)(2,1)} %bitcast.22), calls=%async_computation.3 | async-start | bytes 4194304 | tf_op jit(solution)/shard_map/all_to_all | solution.py:55
  90.0 148.4 %all-gather.9.cloned.1.call-start = ((), (), s32[]{:S(2)}) async-start(), calls=%async_computation.10 | async-start | bytes 10485760 | tf_op jit(solution)/shard_map/all_gather | solution.py:64
  120.0 3.7 copy-start.1
  126.8 11.2 %all-to-all-start.1 = ((s32[32,1,32]{2,1,0:T(1,128)}), s32[32,1,32]{2,1,0:T(1,128)S(1)}, u32[]{:S(2)}, u32[]{:S(2)}) async-start(s32[32,1,32]{2,1,0:T(1,128)} %all_to_all.37), calls=%async_computation.1 | async-start | bytes 32768 | tf_op jit(solution)/shard_map/all_to_all | solution.py:56
  138.0 34.8 %all-to-all-start = ((bf16[32,32,1024]{2,1,0:T(8,128)(2,1)}), bf16[32,32,1024]{2,1,0:T(8,128)(2,1)S(1)}, u32[]{:S(2)}, u32[]{:S(2)}) async-start(bf16[32,32,1024]{2,1,0:T(8,128)(2,1)} %bitcast.7), calls=%async_computation | async-start | bytes 4194304 | tf_op jit(solution)/shard_map/all_to_all | solution.py:55
  142.9 181.2 %all-gather.7.cloned.1.call-start = ((), (), s32[]{:S(2)}) async-start(), calls=%async_computation.9 | async-start | bytes 10485760 | tf_op jit(solution)/shard_map/all_gather | solution.py:64
  172.8 3.7 copy-start.2
  203.4 150.2 %all-to-all-start.2 = ((bf16[32,32,1024]{2,1,0:T(8,128)(2,1)}), bf16[32,32,1024]{2,1,0:T(8,128)(2,1)S(1)}, u32[]{:S(2)}, u32[]{:S(2)}) async-start(bf16[32,32,1024]{2,1,0:T(8,128)(2,1)} %subtract_convert_fusion.2), calls=%async_computation.2 | async-start | bytes 4194304 | tf_op jit(solution)/shard_map/all_to_all | solution.py:48
  353.5 37.4 %all-to-all-start.8 = ((bf16[32,32,1024]{2,1,0:T(8,128)(2,1)}), bf16[32,32,1024]{2,1,0:T(8,128)(2,1)}, u32[]{:S(2)}, u32[]{:S(2)}) async-start(bf16[32,32,1024]{2,1,0:T(8,128)(2,1)} %subtract_convert_fusion), calls=%async_computation.8 | async-start | bytes 4194304 | tf_op jit(solution)/shard_map/all_to_all | solution.py:48
  391.0 34.7 %all-to-all-start.5 = ((bf16[32,32,1024]{2,1,0:T(8,128)(2,1)}), bf16[32,32,1024]{2,1,0:T(8,128)(2,1)}, u32[]{:S(2)}, u32[]{:S(2)}) async-start(bf16[32,32,1024]{2,1,0:T(8,128)(2,1)} %subtract_convert_fusion.1), calls=%async_computation.5 | async-start | bytes 4194304 | tf_op jit(solution)/shard_map/all_to_all | solution.py:48
Sparse Core Ops, SparseCore 0:
  70.6 81.4 all-gather.10
  153.8 84.4 all-gather.8
  240.0 83.9 all-gather.6
